TPU v7x, 32 devices: a whole 2x2x4 slice. The times are simulated.
32 devices in a mesh: tok: 16 (over z, x, core), lyr: 2 (over y).
Axes of the slice: x: 2, y: 2, z: 4, core: 2. Of those that a mesh axis runs over, the one named last changes fastest.
Arguments:
- feature_codes: bfloat16 [4, 2048, 2, 256], P('lyr', 'tok'), may hold values from 0 to 21, as said below
- block_ids: int32 [4, 2048, 2], P('lyr', 'tok'), may hold values from 0 to 31, all different within a row; in each aligned block of 128 rows (0 to 127, 128 to 255, ..., all dimensions but the last counted through in order) at most 16 rows name the same one
- target_layer: int32 [2048], P('tok'), may hold values from 0 to 3
- request_ids: int32 [2048], P('tok'), may hold values from 0 to 15
- target_resid: bfloat16 [2048, 2304], P('tok'), may hold values from -6 to 6
- decoder: bfloat16 [4, 8192, 2304], P('lyr', 'tok'), may hold values from -0.25 to 0.25
Outputs:
- scores: bfloat16 [4, 2048, 2, 256], P('lyr', 'tok')
- request_totals: float32 [16, 4, 8192], P(None, 'lyr', 'tok')
Inputs may be any that keep to these rules, and one draw needn't show every extreme that they name: `block_ids`: the 2 panel indices of one token at one source layer are distinct; among the 128 tokens of one index of tok at one source layer no panel is named by more than 16 of them, a bound that some block reaches. `feature_codes`: nonnegative, with many entries zero.
All inputs are finite; a program needn't handle non-finite values.
Results may differ from a plain program's by a relative error of at most 0.0053.
Values may be sent and summed in bfloat16 or wider, within the bound.
A program may use at most 64 MiB of HBM per device.

v0:
```python
import functools

import jax
import jax.numpy as jnp
from jax import lax
from jax.experimental import pallas as pl
from jax.experimental.pallas import tpu as pltpu
from jax.sharding import PartitionSpec as P

REQUESTS = 16
CAP = 16
MESH = pl.DeviceIdType.MESH


class Place:
    def __init__(self):
        tok, y = lax.axis_index("tok"), lax.axis_index("lyr")
        z, x, c = tok // 4, (tok // 2) % 2, tok % 2
        self.z, self.c = z, c
        self.inner = (z % 3) != 0
        self.first = (1 - c) * y + c * x
        self.second = (1 - c) * x + c * y
        across_x, across_y = (tok + 2 - 4 * x, y), (tok, 1 - y)
        self.to_first = tuple((1 - c) * a + c * b for a, b in zip(across_y, across_x))
        self.to_second = tuple((1 - c) * a + c * b for a, b in zip(across_x, across_y))
        self.to_core = (tok + 1 - 2 * c, y)
        self.tok, self.y = tok, y
        half = z // 2
        self.near = [z, z + 1 - 2 * (z % 2), 2 - half, 3 - 3 * half]

    def along(self, step):
        return (self.tok + 4 * step, self.y)

    def quarter(self, first, second):
        return (1 - self.c) * (second * 2 + first) + self.c * (first * 2 + second)

    def peer(self, distance):
        return ((self.tok + distance) % 16, self.y)

    def barrier(self):
        gate = pltpu.get_barrier_semaphore()
        for distance in range(1, 16):
            pl.semaphore_signal(gate, inc=1, device_id=self.peer(distance), device_id_type=MESH)
        pl.semaphore_signal(gate, inc=1, device_id=(self.tok, 1 - self.y), device_id_type=MESH)
        pl.semaphore_wait(gate, 16)


def earlier(count):
    shape = (count, count)
    return (lax.broadcasted_iota(jnp.int32, shape, 0) < lax.broadcasted_iota(jnp.int32, shape, 1)).astype(jnp.bfloat16)


def slots(numbers, layer, first_panel, panels):
    shape = (panels * CAP, numbers.shape[1])
    row = lax.broadcasted_iota(jnp.int32, shape, 0)
    panel = row // CAP + first_panel
    rank = (row % CAP).astype(jnp.float32)
    named = [numbers[2 * layer + k : 2 * layer + k + 1] == panel for k in (0, 1)]
    either = jnp.where(named[0] | named[1], 1.0, 0.0).astype(jnp.bfloat16)
    before = jnp.dot(either, earlier(shape[1]), preferred_element_type=jnp.float32)
    here = before == rank
    return [jnp.where(n & here, 1.0, 0.0).astype(jnp.bfloat16) for n in named]


def remote(src, dst, send, recv, target):
    return pltpu.make_async_remote_copy(
        src_ref=src, dst_ref=dst, send_sem=send, recv_sem=recv, device_id=target, device_id_type=MESH
    )


def gather_kernel(
    own_ref, dense_ref, weights_ref, numbers_ref, hot_ref, sent_ref, scores_ref, totals_ref,
    out_ref, slot_out, slot_in, local_sem, recv_sem, core_sem, first_sem, second_sem, z_sem, slot_send, slot_recv,
):
    at = Place()
    at.barrier()

    def block(z, first, second, core):
        return (z * 2 + core) * 4 + at.quarter(first, second)

    def mine(j, flip_first, flip_second):
        f = 1 - at.first if flip_first else at.first
        s = 1 - at.second if flip_second else at.second
        return block(at.near[j], f, s, at.c)

    def send(b, sem, target):
        remote(out_ref.at[b], out_ref.at[b], sem, recv_sem.at[b], target).start()

    def arrived(b):
        remote(out_ref.at[b], out_ref.at[b], core_sem.at[0], recv_sem.at[b], at.to_core).wait_recv()

    b0 = mine(0, False, False)
    keep = pltpu.make_async_copy(own_ref, out_ref.at[b0], local_sem)
    keep.start()
    keep.wait()
    used = [0, 0, 0]

    def fan(b, second, first):
        if second:
            send(b, second_sem.at[used[1]], at.to_second)
            used[1] += 1
        if first:
            send(b, first_sem.at[used[0]], at.to_first)
            used[0] += 1
        send(b, core_sem.at[used[2]], at.to_core)
        used[2] += 1

    @pl.when(at.z > 0)
    def _():
        send(b0, z_sem.at[0], at.along(-1))

    @pl.when(at.z < 3)
    def _():
        send(b0, z_sem.at[1], at.along(1))

    fan(b0, True, True)

    def from_z(j):
        b = mine(j, False, False)
        arrived(b)
        step = (3 - 2 * at.z) if j == 1 else (2 * at.z - 3)

        @pl.when(at.inner)
        def _():
            send(b, z_sem.at[1 + j], at.along(step))

        fan(b, True, True)

    def from_second(j):
        b = mine(j, False, True)
        arrived(b)
        fan(b, False, True)

    def from_first(j, flip):
        b = mine(j, True, flip)
        arrived(b)
        fan(b, False, False)

    rows = out_ref.shape[1]
    panel = slot_out.shape[-1]
    totals_ref[...] = jnp.zeros_like(totals_ref)

    def slot_copy(source):
        return remote(
            slot_out.at[source], slot_in.at[at.tok], slot_send.at[source], slot_recv.at[at.tok], (source, at.y)
        )

    def project(z, core, own):
        group = z * 2 + core
        left = out_ref[pl.ds(group * 4, 4)].reshape(4 * rows, out_ref.shape[2])
        sources = [(z * 2 + x) * 2 + core for x in (0, 1)]
        numbers = [numbers_ref[source] for source in sources]
        members = []
        for x in (0, 1):
            wanted = lax.broadcasted_iota(jnp.int32, (REQUESTS, 2 * rows), 0)
            members.append(jnp.where(numbers[x][4:5] == wanted, 1.0, 0.0).astype(jnp.bfloat16))
        for n in range(4):
            layer, which = n // 2, n % 2
            cols = slice(n * panel, (n + 1) * panel)
            product = lax.dot_general(
                left, weights_ref[cols, :], (((1,), (1,)), ((), ())), preferred_element_type=jnp.float32
            ).astype(jnp.bfloat16)
            for x in (0, 1):
                span = slice(x * 2 * rows, (x + 1) * 2 * rows)
                value = product[span].astype(jnp.float32) * dense_ref[group, x, :, cols].astype(jnp.float32)
                high = value.astype(jnp.bfloat16)
                low = (value - high.astype(jnp.float32)).astype(jnp.bfloat16)
                totals_ref[:, cols] += jnp.dot(members[x], high, preferred_element_type=jnp.float32) + jnp.dot(
                    members[x], low, preferred_element_type=jnp.float32
                )
                hot = hot_ref[sources[x], layer, which * CAP : (which + 1) * CAP, :]
                packed = jnp.dot(hot, high, preferred_element_type=jnp.float32).astype(jnp.bfloat16)
                slot_out[sources[x], layer, which * CAP : (which + 1) * CAP, :] = packed
        for x in (0, 1):
            if own:

                @pl.when(sources[x] != at.tok)
                def _():
                    slot_copy(sources[x]).start()

            else:
                slot_copy(sources[x]).start()

    def from_core(j):
        for q in range(4):
            arrived((at.near[j] * 2 + 1 - at.c) * 4 + q)
        project(at.near[j], 1 - at.c, False)

    from_second(0)
    from_z(1)
    from_first(0, False)
    from_second(1)
    from_z(2)
    from_first(0, True)
    from_first(1, False)
    from_second(2)
    from_z(3)
    from_first(1, True)
    from_first(2, False)
    from_second(3)
    project(at.near[0], at.c, True)
    from_core(0)
    project(at.near[1], at.c, False)
    from_first(2, True)
    project(at.near[2], at.c, False)
    from_first(3, False)
    from_core(1)
    from_first(3, True)
    from_core(2)
    project(at.near[3], at.c, False)
    from_core(3)
    slot_in[at.tok] = slot_out[at.tok]
    for distance in range(1, 16):
        source = (at.tok + distance) % 16
        remote(
            slot_out.at[0], slot_in.at[source], slot_send.at[0], slot_recv.at[source], at.to_core
        ).wait_recv()
    for layer in (0, 1):
        table = slot_in[:, layer].reshape(32 * CAP, panel)
        for k in (0, 1):
            scores_ref[2 * layer + k] = lax.dot_general(
                sent_ref[2 * layer + k], table, (((0,), (0,)), ((), ())), preferred_element_type=jnp.float32
            ).astype(scores_ref.dtype)
    for distance in range(1, 16):
        source = (at.tok + distance) % 16
        remote(
            slot_out.at[0], slot_in.at[0], slot_send.at[source], slot_recv.at[0], at.to_core
        ).wait_send()
    for i in range(16):
        remote(own_ref, own_ref, core_sem.at[i], recv_sem.at[0], at.to_core).wait_send()
    for i in range(8):
        remote(own_ref, own_ref, first_sem.at[i], recv_sem.at[0], at.to_core).wait_send()
    for i in range(4):
        remote(own_ref, own_ref, second_sem.at[i], recv_sem.at[0], at.to_core).wait_send()

    @pl.when(at.z > 0)
    def _():
        remote(own_ref, own_ref, z_sem.at[0], recv_sem.at[0], at.to_core).wait_send()

    @pl.when(at.z < 3)
    def _():
        remote(own_ref, own_ref, z_sem.at[1], recv_sem.at[0], at.to_core).wait_send()

    @pl.when(at.inner)
    def _():
        for i in range(2, 5):
            remote(own_ref, own_ref, z_sem.at[i], recv_sem.at[0], at.to_core).wait_send()


def gather_rows(own, dense, weights, numbers, hot, sent, panel):
    rows, width = own.shape
    dma, bf16 = pltpu.SemaphoreType.DMA, jnp.bfloat16
    vmem = pl.BlockSpec(memory_space=pltpu.VMEM)
    return pl.pallas_call(
        gather_kernel,
        out_shape=(
            jax.ShapeDtypeStruct((4, 2 * rows, panel), bf16),
            jax.ShapeDtypeStruct((REQUESTS, weights.shape[0]), jnp.float32),
        ),
        in_specs=[vmem] * 6,
        out_specs=(vmem, vmem),
        scratch_shapes=[
            pltpu.VMEM((32, rows, width), bf16),
            pltpu.VMEM((16, 2, 2 * CAP, panel), bf16),
            pltpu.VMEM((16, 2, 2 * CAP, panel), bf16),
            dma, dma((32,)), dma((16,)), dma((8,)), dma((4,)), dma((5,)), dma((16,)), dma((16,)),
        ],
        compiler_params=pltpu.CompilerParams(
            collective_id=1, has_side_effects=True, vmem_limit_bytes=60 * 1024 * 1024
        ),
        name="gather_rows",
    )(own, dense, weights, numbers, hot, sent)


def reduce_kernel(
    masked_ref, local_numbers_ref, weights_ref, resid_ref,
    out_ref, codes_ref, numbers_ref, hot_ref, sent_ref,
    packed, slot_in, slot_send, slot_recv, number_send, number_recv, held, core_out, core_in, first_out, first_in, second_out, second_in, z_out, z_in,
    core_send, core_recv, first_send, first_recv, second_send, second_recv, z_send, z_recv,
):
    at = Place()
    at.barrier()
    rows, width = out_ref.shape
    depth = codes_ref.shape[-1]
    panel = packed.shape[-1]
    far = at.near[::-1]
    local = local_numbers_ref[...]
    numbers_ref[at.tok] = local
    for layer in (0, 1):
        sent = slots(local, layer, 0, 32)
        for k in (0, 1):
            sent_ref[2 * layer + k] = sent[k]
        value = sum(
            jnp.dot(sent[k], masked_ref[2 * layer + k], preferred_element_type=jnp.float32) for k in (0, 1)
        )
        packed[:, layer] = value.astype(packed.dtype).reshape(16, 2 * CAP, panel)

    def peers(i):
        return [far[i] * 4 + (at.tok + step) % 4 for step in range(1 if i == 3 else 0, 4)]

    def slot_copies(target, source):
        return (
            remote(packed.at[target], slot_in.at[source], slot_send.at[target], slot_recv.at[source], (target, at.y)),
            remote(
                local_numbers_ref, numbers_ref.at[source], number_send.at[target], number_recv.at[source],
                (target, at.y),
            ),
        )

    for i in range(4):
        for target in peers(i):
            for copy in slot_copies(target, at.tok):
                copy.start()
    slot_in[at.tok] = packed[at.tok]

    def unpack(i):
        for source in peers(i):
            for copy in slot_copies(source, source):
                copy.wait_recv()

        @pl.loop(0, 4)
        def _(step):
            source = far[i] * 4 + step
            for layer in (0, 1):
                held_slots = slots(numbers_ref[source], layer, at.tok * 2, 2)
                hot = held_slots[0] + held_slots[1]
                hot_ref[source, layer] = hot
                for which in (0, 1):
                    part = slice(which * CAP, (which + 1) * CAP)
                    n = 2 * layer + which
                    codes_ref[far[i] * 2 + step % 2, step // 2, :, n * panel : (n + 1) * panel] = (
                        lax.dot_general(
                            hot[part], slot_in[source, layer, part, :], (((0,), (0,)), ((), ())),
                            preferred_element_type=jnp.float32,
                        ).astype(codes_ref.dtype)
                    )

    tile = 256 if width % 256 == 0 else width

    def product(i):
        unpack(i)
        for core in (1 - at.c, at.c):
            left = codes_ref[far[i] * 2 + core].reshape(4 * rows, depth)
            away = core is not at.c

            @pl.loop(0, width // tile)
            def _(n):
                cols = pl.ds(pl.multiple_of(n * tile, tile), tile)
                value = jnp.dot(left, weights_ref[:, cols], preferred_element_type=jnp.float32)
                value = value.reshape(4, rows, tile)
                if away:
                    core_out[i, :, :, cols] = value.astype(core_out.dtype)
                else:
                    held[i, :, :, cols] = value

            if away:
                core_copy(i).start()

    def core_copy(i):
        return remote(core_out.at[i], core_in.at[i], core_send.at[i], core_recv.at[i], at.to_core)

    def first_copy(i, k):
        return remote(first_out.at[i, k], first_in.at[i, k], first_send.at[i, k], first_recv.at[i, k], at.to_first)

    def second_copy(i):
        return remote(second_out.at[i], second_in.at[i], second_send.at[i], second_recv.at[i], at.to_second)

    def z_copy(i, way, step):
        slot = way * 4 + far[i]
        return remote(z_out.at[i], z_in.at[slot], z_send.at[i], z_recv.at[slot], at.along(step))

    def f32(v):
        return v.astype(jnp.float32)

    def both(i, q):
        return held[i, q] + f32(core_in[i, q])

    def spot(k):
        return 1 - at.second if k == 0 else at.second

    def over_first(i):
        core_copy(i).wait_recv()
        for k in (0, 1):
            first_out[i, k] = both(i, at.quarter(1 - at.first, spot(k))).astype(first_out.dtype)
            first_copy(i, k).start()

    def over_second(i):
        first_copy(i, 0).wait_recv()
        total = both(i, at.quarter(at.first, spot(0))) + f32(first_in[i, 0])
        second_out[i] = total.astype(second_out.dtype)
        second_copy(i).start()

    def z_arrived(slot):
        remote(z_in.at[slot], z_in.at[slot], z_send.at[0], z_recv.at[slot], at.to_core).wait_recv()

    def along_z(i):
        first_copy(i, 1).wait_recv()
        second_copy(i).wait_recv()
        q = at.quarter(at.first, at.second)
        total = both(i, q) + f32(first_in[i, 1]) + f32(second_in[i])
        held[i, q] = total
        if i < 3:
            way = (at.z // 2) if i < 2 else (at.z % 2)
            slot = way * 4 + far[i]

            @pl.when(at.inner)
            def _():
                z_arrived(slot)
                z_out[i] = (held[i, q] + f32(z_in[slot])).astype(z_out.dtype)

            @pl.when(jnp.logical_not(at.inner))
            def _():
                z_out[i] = held[i, q].astype(z_out.dtype)

            z_copy(i, way, 1 - 2 * way).start()
        else:
            @pl.when(at.z > 0)
            def _():
                z_arrived(at.z)
                held[i, q] += f32(z_in[at.z])

            @pl.when(at.z < 3)
            def _():
                z_arrived(4 + at.z)
                held[i, q] += f32(z_in[4 + at.z])

            error = f32(resid_ref[...]) - held[i, q]
            spread = jnp.mean(error * error, axis=-1, keepdims=True)
            out_ref[...] = (error * lax.rsqrt(spread + 1e-06)).astype(out_ref.dtype)

    product(0)
    over_first(0)
    product(1)
    over_first(1)
    over_second(0)
    product(2)
    over_first(2)
    over_second(1)
    along_z(0)
    product(3)
    over_first(3)
    over_second(2)
    along_z(1)
    over_second(3)
    along_z(2)
    along_z(3)
    for i in range(4):
        for target in peers(i):
            for copy in slot_copies(target, target):
                copy.wait_send()
    for i in range(4):
        core_copy(i).wait_send()
        first_copy(i, 0).wait_send()
        first_copy(i, 1).wait_send()
        second_copy(i).wait_send()
        if i < 3:
            remote(z_out.at[i], z_out.at[i], z_send.at[i], z_recv.at[0], at.to_core).wait_send()


def reduce_rows(masked, local_numbers, weights, resid):
    rows, width = resid.shape
    depth = weights.shape[0]
    panel = masked.shape[-1]
    dma, bf16 = pltpu.SemaphoreType.DMA, jnp.bfloat16
    vmem = pl.BlockSpec(memory_space=pltpu.VMEM)
    block = (rows, width)
    return pl.pallas_call(
        reduce_kernel,
        out_shape=(
            jax.ShapeDtypeStruct(block, bf16),
            jax.ShapeDtypeStruct((8, 2, 2 * rows, depth), bf16),
            jax.ShapeDtypeStruct((16,) + local_numbers.shape, jnp.int32),
            jax.ShapeDtypeStruct((16, 2, 2 * CAP, 2 * rows), bf16),
            jax.ShapeDtypeStruct((4, 32 * CAP, 2 * rows), bf16),
        ),
        in_specs=[vmem] * 4,
        out_specs=(vmem,) * 5,
        scratch_shapes=[
            pltpu.VMEM((16, 2, 2 * CAP, panel), bf16),
            pltpu.VMEM((16, 2, 2 * CAP, panel), bf16),
            dma((16,)), dma((16,)), dma((16,)), dma((16,)),
            pltpu.VMEM((4, 4) + block, jnp.float32),
            pltpu.VMEM((4, 4) + block, bf16),
            pltpu.VMEM((4, 4) + block, bf16),
            pltpu.VMEM((4, 2) + block, bf16),
            pltpu.VMEM((4, 2) + block, bf16),
            pltpu.VMEM((4,) + block, bf16),
            pltpu.VMEM((4,) + block, bf16),
            pltpu.VMEM((3,) + block, bf16),
            pltpu.VMEM((8,) + block, bf16),
            dma((4,)), dma((4,)), dma((4, 2)), dma((4, 2)), dma((4,)), dma((4,)), dma((3,)), dma((8,)),
        ],
        compiler_params=pltpu.CompilerParams(
            collective_id=2, has_side_effects=True, vmem_limit_bytes=60 * 1024 * 1024
        ),
        name="reduce_rows",
    )(masked, local_numbers, weights, resid)


def per_device(feature_codes, block_ids, target_layer, request_ids, target_resid, decoder, grid=False):
    layers_here, count, kact, panel = feature_codes.shape
    width = target_resid.shape[1]
    features = decoder.shape[1]
    per_dev = features // panel
    tok, lyr = lax.axis_index("tok"), lax.axis_index("lyr")
    lyr_count = lax.axis_size("lyr")
    layer_ids = lyr * layers_here + jnp.arange(layers_here, dtype=jnp.int32)
    alive = layer_ids[:, None] <= target_layer[None, :]
    masked = jnp.where(alive[:, :, None, None], feature_codes, jnp.zeros_like(feature_codes))
    numbers = jnp.concatenate(
        [jnp.moveaxis(block_ids, 1, 2).reshape(layers_here * kact, count), request_ids[None, :]], axis=0
    )
    weights = decoder.reshape(layers_here * features, width)
    rows = count // lyr_count
    resid = lax.dynamic_slice_in_dim(target_resid, lyr * rows, rows, 0)
    if grid:
        numbers = jnp.concatenate([numbers, jnp.zeros((8 - numbers.shape[0], count), jnp.int32)], axis=0)
        by_k = jnp.moveaxis(masked, 1, 2).reshape(layers_here * kact, count, panel)
        gradient, *rest = reduce_rows(by_k, numbers, weights, resid)
        dense, all_numbers, hot, sent = rest
        scores, totals = gather_rows(gradient, dense, weights, all_numbers, hot, sent, panel)
        scores = jnp.moveaxis(scores.reshape(layers_here, kact, count, panel), 1, 2)
        return (scores, totals.reshape(REQUESTS, layers_here, features))
    all_codes = lax.all_gather(masked, "tok", axis=1, tiled=True)
    numbers = lax.all_gather(numbers, "tok", axis=1, tiled=True)
    all_ids = jnp.moveaxis(numbers[:-1].reshape(layers_here, kact, -1), 1, 2)
    all_requests = numbers[-1]
    mine = tok * per_dev + jnp.arange(per_dev, dtype=jnp.int32)
    named = (all_ids[..., None] == mine).astype(jnp.bfloat16)
    dense = jnp.sum(all_codes[:, :, :, None, :] * named[..., None], axis=2)
    tokens = dense.shape[1]
    dense = jnp.swapaxes(dense, 0, 1).reshape(tokens, layers_here * features)
    partial = jnp.dot(dense, weights, preferred_element_type=jnp.float32).astype(jnp.bfloat16)
    rebuilt = lax.psum_scatter(partial, ("tok", "lyr"), scatter_dimension=0, tiled=True)
    error = resid.astype(jnp.float32) - rebuilt.astype(jnp.float32)
    spread = jnp.mean(error * error, axis=-1, keepdims=True)
    gradient = (error * lax.rsqrt(spread + 1e-06)).astype(jnp.bfloat16)
    gradients = lax.all_gather(gradient, ("tok", "lyr"), axis=0, tiled=True)
    projected = lax.dot_general(
        gradients, weights, (((1,), (1,)), ((), ())), preferred_element_type=jnp.float32
    ).astype(jnp.bfloat16)
    attribution = dense.astype(jnp.float32) * projected.astype(jnp.float32)
    members = (all_requests[:, None] == jnp.arange(REQUESTS, dtype=jnp.int32)).astype(jnp.float32)
    totals = lax.dot_general(
        members, attribution, (((0,), (0,)), ((), ())), precision=lax.Precision.HIGHEST
    ).reshape(REQUESTS, layers_here, features)
    scored = attribution.astype(jnp.bfloat16).reshape(tokens, layers_here, 1, per_dev, panel)
    spread_out = jnp.sum(
        scored * jnp.swapaxes(named, 0, 1)[..., None], axis=3
    )
    scores = lax.psum_scatter(
        jnp.swapaxes(spread_out, 0, 1), "tok", scatter_dimension=1, tiled=True
    )
    return (scores, totals)


def solution(mesh):
    placed = (
        P("lyr", "tok", None, None),
        P("lyr", "tok", None),
        P("tok"),
        P("tok"),
        P("tok", None),
        P("lyr", "tok", None),
    )
    wide = len({getattr(d, "coords", (0,))[0] for d in mesh.devices.flat})
    grid = (mesh.shape["tok"], mesh.shape["lyr"]) == (16, 2) and wide == 2
    return jax.shard_map(
        functools.partial(per_device, grid=grid),
        mesh=mesh,
        in_specs=placed,
        out_specs=(P("lyr", "tok", None, None), P(None, "lyr", "tok")),
        check_vma=False,
    )
```

profile of v0, /device:TPU:0, one launch (start us, length us, event | category | flops | bytes accessed | tf_op | source)
XLA Modules:
  0.0 163.2 jit_solution(4595222512565337545)
XLA Ops:
  0.6 0.0 copy-start
  0.7 0.8 broadcast_compare_fusion
  1.4 0.1 pad.2.clone
  1.5 1.4 add_add_fusion.local_numbers_ref
  2.9 1.4 fusion
  4.3 0.7 copy.8
  5.0 0.0 copy-done
  5.0 0.7 constant_dynamic-slice_fusion.resid_ref
  5.8 75.8 %reduce_rows.1 = (bf16[64,2304]{1,0:T(8,128)(2,1)}, bf16[8,2,128,1024]{3,2,1,0:T(8,128)(2,1)}, s32[16,8,128]{2,1,0:T(8,128)}, bf16[16,2,32,128]{3,2,1,0:T(8,128)(2,1)}, bf16[4,512,128]{2,1,0:T(8,128)(2,1)}) custom-call(bf16[4,128,256]{2,1,0:T(8,128)(2,1)} %bitcast.14, s32[8,128]{1,0:T(8,128)} %add_add_fusion.local_numbers_ref, bf16[1024,2304]{1,0:T(8,128)(2,1)} %bitcast.12, ...), custom_call_target="tpu_custom_call" | custom-call | tf_op jit(solution)/shard_map/reduce_rows/pallas_call | solution.py:467
  81.6 78.1 %gather_rows.1 = (bf16[4,128,256]{2,1,0:T(8,128)(2,1)}, f32[16,1024]{1,0:T(8,128)}) custom-call(bf16[64,2304]{1,0:T(8,128)(2,1)} %get-tuple-element.9.own_ref, bf16[8,2,128,1024]{3,2,1,0:T(8,128)(2,1)} %get-tuple-element.10.dense_ref, bf16[1024,2304]{1,0:T(8,128)(2,1)} %bitcast.13, s32[16,8,128]{2,1,0:T(8,128)} %get-tuple-element.11.numbers_ref, ...), custom_call_target="tpu_custom_call" | custom-call | tf_op jit(solution)/shard_map/gather_rows/pallas_call | solution.py:254
  159.7 1.9 %copy.11 = bf16[2,2,128,256]{3,1,2,0:T(2,128)(2,1)} copy(bf16[2,2,128,256]{3,2,1,0:T(8,128)(2,1)} %bitcast.16) | data formatting | bytes 524288 | tf_op jit(solution)/shard_map/reshape | solution.py:522
  161.6 1.5 reshape.53
  (2 shorter events, 0.0 us)
Async XLA Ops:
  0.6 4.4 %copy-start = (bf16[128,2304]{1,0:T(8,128)(2,1)S(1)}, bf16[128,2304]{1,0:T(8,128)(2,1)}, u32[]{:S(2)}) copy-start(bf16[128,2304]{1,0:T(8,128)(2,1)} %param.10) | copy-start | bytes 1769476
where the time goes:
time: 164 us; the launch traced here: 163 us
  Pallas kernels  154 us (94%)
  local copies, waits for them, and re-layouts  5.01 us (3%)
  other arithmetic  3.54 us (2%)
    pallas_call x1, Pallas kernels, gather_rows(): pl.pallas_call(gather_kernel, out_shape=(jax.ShapeDtypeStruct((4, 2 * row...  78.1 us
    pallas_call x1, Pallas kernels, reduce_rows(): pl.pallas_call(reduce_kernel, out_shape=(jax.ShapeDtypeStruct(block, bf16...  75.8 us

commit v1 on v0

v1 whole, which is shorter than its diff:
```python
import functools

import jax
import jax.numpy as jnp
from jax import lax
from jax.experimental import pallas as pl
from jax.experimental.pallas import tpu as pltpu
from jax.sharding import PartitionSpec as P

REQUESTS = 16
CAP = 16
WAVES = 2
MESH = pl.DeviceIdType.MESH


class Place:
    def __init__(self):
        tok, y = lax.axis_index("tok"), lax.axis_index("lyr")
        z, x, c = tok // 4, (tok // 2) % 2, tok % 2
        self.z, self.c = z, c
        self.inner = (z % 3) != 0
        self.first = (1 - c) * y + c * x
        self.second = (1 - c) * x + c * y
        across_x, across_y = (tok + 2 - 4 * x, y), (tok, 1 - y)
        self.to_first = tuple((1 - c) * a + c * b for a, b in zip(across_y, across_x))
        self.to_second = tuple((1 - c) * a + c * b for a, b in zip(across_x, across_y))
        self.to_core = (tok + 1 - 2 * c, y)
        self.tok, self.y = tok, y
        half = z // 2
        self.near = [z, z + 1 - 2 * (z % 2), 2 - half, 3 - 3 * half]

    def along(self, step):
        return (self.tok + 4 * step, self.y)

    def quarter(self, first, second):
        return (1 - self.c) * (second * 2 + first) + self.c * (first * 2 + second)

    def peer(self, distance):
        return ((self.tok + distance) % 16, self.y)

    def greet(self):
        gate = pltpu.get_barrier_semaphore()
        for distance in range(1, 16):
            pl.semaphore_signal(gate, inc=1, device_id=self.peer(distance), device_id_type=MESH)
        pl.semaphore_signal(gate, inc=1, device_id=(self.tok, 1 - self.y), device_id_type=MESH)

    def meet(self):
        pl.semaphore_wait(pltpu.get_barrier_semaphore(), 16)


def remote(src, dst, send, recv, target):
    return pltpu.make_async_remote_copy(
        src_ref=src, dst_ref=dst, send_sem=send, recv_sem=recv, device_id=target, device_id_type=MESH
    )


def f32(value):
    return value.astype(jnp.float32)


def ones(where):
    return jnp.where(where, 1.0, 0.0).astype(jnp.bfloat16)


def rows_of(shape):
    return lax.broadcasted_iota(jnp.int32, shape, 0)


def lanes_of(shape):
    return lax.broadcasted_iota(jnp.int32, shape, 1)


def product(left, right, left_dim=1, right_dim=0):
    return lax.dot_general(left, right, (((left_dim,), (right_dim,)), ((), ())), preferred_element_type=jnp.float32)


def transcoder_kernel(
    codes_ref, ids_ref, request_ref, limit_ref, decoder_ref, target_ref, scores_ref, totals_ref,
    weights, resid, packed, slot_in, sent, hot, turned, members, core_out, chip_in, held,
    first_out, first_in, second_out, second_in, z_out, z_in, grads, picked, slot_out, slot_back, low,
    load_sem, code_send, code_recv, core_send, core_recv, first_send, first_recv, second_send, second_recv,
    z_send, z_recv, own_core, own_first, own_second, own_z, block_recv, slot_send, slot_recv,
):
    at = Place()
    at.greet()
    half, width = resid.shape
    tokens = limit_ref.shape[1]
    panel = codes_ref.shape[-1]
    slots = 4 * CAP
    step = half // WAVES
    tile = width // 3 if width % 384 == 0 else width
    tiles = [slice(t, t + tile) for t in range(0, width, tile)]
    load = pltpu.make_async_copy(decoder_ref, weights, load_sem.at[0])
    load.start()
    load_target = pltpu.make_async_copy(
        target_ref.at[pl.ds(pl.multiple_of(at.y * half, half), half)], resid, load_sem.at[1]
    )
    load_target.start()

    def wave(w):
        return pl.ds(w * step, step)

    info = []
    ids = ids_ref[...]
    shape = (tokens, tokens)
    earlier = ones(rows_of(shape) < lanes_of(shape))
    panels = rows_of((32, tokens))
    numbers = []
    for layer in (0, 1):
        named = [ids[2 * layer + k : 2 * layer + k + 1] == panels for k in (0, 1)]
        before = product(ones(named[0] | named[1]), earlier)
        alive = limit_ref[...] >= 2 * at.y + layer
        value = None
        for k in (0, 1):
            rank = jnp.sum(jnp.where(named[k], before, 0.0), axis=0, keepdims=True)
            number = f32(ids[2 * layer + k : 2 * layer + k + 1])
            numbers.append((number, rank))
            code = jnp.where(alive, number * CAP + rank, -1.0)
            spot = ones(f32(rows_of((32 * CAP, tokens))) == code)
            sent[2 * layer + k] = spot
            part = product(spot, codes_ref[2 * layer + k])
            value = part if value is None else value + part
        packed[:, layer * 2 * CAP : (layer + 1) * 2 * CAP, :] = value.astype(packed.dtype).reshape(16, 2 * CAP, panel)
    blank = jnp.zeros((7, tokens), jnp.float32)
    info = jnp.concatenate(
        [n for n, _ in numbers] + [r for _, r in numbers] + [f32(request_ref[...]), blank], axis=0
    )
    info = jnp.concatenate([info] * (panel // tokens), axis=1).astype(packed.dtype)
    for target in range(16):
        packed[target, slots : slots + 16, :] = info
    slot_in[at.tok] = packed[at.tok]
    order = (0, 3, 2, 1)

    def peers(j):
        return [at.near[j] * 4 + (at.tok + s) % 4 for s in range(1 if j == 0 else 0, 4)]

    def code_copy(target, source):
        return remote(packed.at[target], slot_in.at[source], code_send.at[target], code_recv.at[source], (target, at.y))

    at.meet()
    for j in order:
        for target in peers(j):
            code_copy(target, at.tok).start()

    eye = ones(rows_of(shape) == lanes_of(shape))

    def unpack(j):
        for source in peers(j):
            code_copy(source, source).wait_recv()

        @pl.loop(0, 4)
        def _(s):
            source = at.near[j] * 4 + s
            told = f32(slot_in[source, slots : slots + 16, :tokens])
            place = [told[i : i + 1] * CAP + told[4 + i : 5 + i] for i in range(4)]
            for away in (0, 1):
                device = at.tok if away == 0 else at.tok + 1 - 2 * at.c
                row = f32(rows_of((2 * CAP, tokens)) + device * (2 * CAP))
                for layer in (0, 1):
                    start = away * slots + layer * 2 * CAP
                    hot[source, start : start + 2 * CAP, :] = ones(
                        (place[2 * layer] == row) | (place[2 * layer + 1] == row)
                    )
            asks = ones(f32(rows_of(shape)) == told[8:9])
            members[source] = product(hot[source, :slots, :], asks, 1, 1).astype(members.dtype)

        for x in (0, 1):
            source = at.near[j] * 4 + x * 2 + at.c
            turned[2 * j + x] = product(hot[source], eye, 0, 0).astype(turned.dtype)

    def panel_span(n):
        return pl.ds(pl.multiple_of(n * CAP, CAP), CAP)

    def weight_span(n):
        return pl.ds(pl.multiple_of(n * panel, panel), panel)

    def core_copy(j, n):
        return remote(
            core_out.at[j, :, panel_span(n), :], chip_in.at[j, :, panel_span(4 + n), :],
            core_send.at[j, n], core_recv.at[j, n], at.to_core,
        )

    def contribute(j):
        sources = [at.near[j] * 4 + x * 2 + core for core in (1 - at.c, at.c) for x in (0, 1)]

        @pl.loop(0, 4)
        def _(n):
            span = panel_span(n)
            left = jnp.concatenate([slot_in[s, span, :] for s in sources], axis=0)
            for cols in tiles:
                value = product(left, weights[weight_span(n), cols]).astype(core_out.dtype)
                for x in (0, 1):
                    core_out[j, x, span, cols] = value[x * CAP : (x + 1) * CAP]
                    chip_in[j, x, span, cols] = value[(2 + x) * CAP : (3 + x) * CAP]
            core_copy(j, n).start()

    def spot(k):
        return 1 - at.second if k == 0 else at.second

    def combine(j):
        for n in range(4):
            core_copy(j, n).wait_recv()
        for kept in (False, True):
            for k in (0, 1):
                first = at.first if kept else 1 - at.first
                x = (1 - at.c) * spot(k) + at.c * first
                h = (1 - at.c) * first + at.c * spot(k)
                left = turned[2 * j + x, pl.ds(pl.multiple_of(h * half, half), half), :]
                for cols in tiles:
                    value = product(left, chip_in[j, x, :, cols])
                    if kept:
                        held[j, k, :, cols] = value
                    else:
                        first_out[j, k, :, cols] = value.astype(first_out.dtype)

    def first_copy(w, j, k):
        return remote(
            first_out.at[j, k, wave(w)], first_in.at[j, k, wave(w)], first_send.at[w, j, k], first_recv.at[w, j, k],
            at.to_first,
        )

    def second_copy(w, j):
        return remote(
            second_out.at[j, wave(w)], second_in.at[j, wave(w)], second_send.at[w, j], second_recv.at[w, j],
            at.to_second,
        )

    def z_arrived(w, slot):
        remote(
            z_in.at[slot, wave(w)], z_in.at[slot, wave(w)], z_send.at[w, 0], z_recv.at[w, slot], at.to_core
        ).wait_recv()

    def over_first(w, j):
        for k in (0, 1):
            first_copy(w, j, k).start()

    def over_second(w, j):
        first_copy(w, j, 0).wait_recv()
        second_out[j, wave(w)] = (held[j, 0, wave(w)] + f32(first_in[j, 0, wave(w)])).astype(second_out.dtype)
        second_copy(w, j).start()

    def along_z(w, j):
        rows = wave(w)
        first_copy(w, j, 1).wait_recv()
        second_copy(w, j).wait_recv()
        total = held[j, 1, rows] + f32(first_in[j, 1, rows]) + f32(second_in[j, rows])
        if j > 0:
            way = (at.z // 2) if j > 1 else (at.z % 2)
            slot = way * 4 + at.near[j]

            @pl.when(at.inner)
            def _():
                z_arrived(w, slot)
                z_out[j, rows] = (total + f32(z_in[slot, rows])).astype(z_out.dtype)

            @pl.when(jnp.logical_not(at.inner))
            def _():
                z_out[j, rows] = total.astype(z_out.dtype)

            remote(
                z_out.at[j, rows], z_in.at[slot, rows], z_send.at[w, j], z_recv.at[w, slot], at.along(1 - 2 * way)
            ).start()
        else:
            held[j, 1, rows] = total

            @pl.when(at.z > 0)
            def _():
                z_arrived(w, at.z)
                held[j, 1, rows] += f32(z_in[at.z, rows])

            @pl.when(at.z < 3)
            def _():
                z_arrived(w, 4 + at.z)
                held[j, 1, rows] += f32(z_in[4 + at.z, rows])

            error = f32(resid[rows]) - held[j, 1, rows]
            spread = jnp.mean(error * error, axis=-1, keepdims=True)
            grads[mine(0, False, False), rows] = (error * lax.rsqrt(spread + 1e-06)).astype(grads.dtype)
            spread_out(w)

    def block(z, first, second, core):
        return (z * 2 + core) * 4 + at.quarter(first, second)

    def mine(j, flip_first, flip_second):
        f = 1 - at.first if flip_first else at.first
        s = 1 - at.second if flip_second else at.second
        return block(at.near[j], f, s, at.c)

    def send(w, b, sem, target):
        remote(grads.at[b, wave(w)], grads.at[b, wave(w)], sem, block_recv.at[w, b], target).start()

    def arrived(w, b):
        remote(
            grads.at[b, wave(w)], grads.at[b, wave(w)], own_core.at[w, 0], block_recv.at[w, b], at.to_core
        ).wait_recv()

    used = [[0, 0, 0] for _ in range(WAVES)]

    def fan(w, b, second, first):
        if second:
            send(w, b, own_second.at[w, used[w][1]], at.to_second)
            used[w][1] += 1
        if first:
            send(w, b, own_first.at[w, used[w][0]], at.to_first)
            used[w][0] += 1
        send(w, b, own_core.at[w, used[w][2]], at.to_core)
        used[w][2] += 1

    def spread_out(w):
        b = mine(0, False, False)

        @pl.when(at.z > 0)
        def _():
            send(w, b, own_z.at[w, 0], at.along(-1))

        @pl.when(at.z < 3)
        def _():
            send(w, b, own_z.at[w, 1], at.along(1))

        fan(w, b, True, True)

    def from_z(w, j):
        b = mine(j, False, False)
        arrived(w, b)
        onward = (3 - 2 * at.z) if j == 1 else (2 * at.z - 3)

        @pl.when(at.inner)
        def _():
            send(w, b, own_z.at[w, 1 + j], at.along(onward))

        fan(w, b, True, True)

    def from_second(w, j):
        b = mine(j, False, True)
        arrived(w, b)
        fan(w, b, False, True)

    def from_first(w, j, flip):
        b = mine(j, True, flip)
        arrived(w, b)
        fan(w, b, False, False)

    def from_core(w, j):
        for q in range(4):
            arrived(w, (at.near[j] * 2 + 1 - at.c) * 4 + q)

    def slot_copy(target, source):
        return remote(
            slot_out.at[target], slot_back.at[source], slot_send.at[target], slot_recv.at[source], (target, at.y)
        )

    def pick(j, core):
        for x in (0, 1):
            source = at.near[j] * 4 + x * 2 + core
            rows = grads[pl.ds((at.near[j] * 2 + core) * 4 + 2 * x, 2)].reshape(tokens, width)
            for cols in tiles:
                value = product(hot[source, :slots, :], rows[:, cols]).astype(picked.dtype)
                for n in range(4):
                    picked[n, x * CAP : (x + 1) * CAP, cols] = value[n * CAP : (n + 1) * CAP]

    def project(j, core):
        pick(j, core)
        sources = [at.near[j] * 4 + x * 2 + core for x in (0, 1)]

        @pl.loop(0, 4)
        def _(n):
            span = panel_span(n)
            value = f32(product(picked[n], weights[weight_span(n), :], 1, 1).astype(jnp.bfloat16))
            value = value * f32(jnp.concatenate([slot_in[s, span, :] for s in sources], axis=0))
            high = value.astype(jnp.bfloat16)
            rest = (value - f32(high)).astype(jnp.bfloat16)
            for x in (0, 1):
                slot_out[sources[x], span, :] = high[x * CAP : (x + 1) * CAP]
                low[sources[x], span, :] = rest[x * CAP : (x + 1) * CAP]

        for source in sources:
            if j == 0:

                @pl.when(source != at.tok)
                def _():
                    slot_copy(source, at.tok).start()

            else:
                slot_copy(source, at.tok).start()

    unpack(0)
    load.wait()
    contribute(0)
    combine(0)
    for w in range(WAVES):
        over_first(w, 0)
    unpack(3)
    contribute(3)
    combine(3)
    over_first(0, 3)
    over_second(0, 0)
    unpack(2)
    contribute(2)
    combine(2)
    over_first(0, 2)
    over_second(0, 3)
    unpack(1)
    contribute(1)
    combine(1)
    over_first(0, 1)
    load_target.wait()
    over_first(1, 3)
    over_second(0, 2)
    along_z(0, 3)
    over_second(1, 0)
    over_first(1, 2)
    over_second(0, 1)
    along_z(0, 2)
    over_first(1, 1)
    along_z(0, 1)
    over_second(1, 3)
    along_z(0, 0)
    over_second(1, 2)
    along_z(1, 3)
    from_second(0, 0)
    from_z(0, 1)
    over_second(1, 1)
    along_z(1, 2)
    from_first(0, 0, False)
    from_second(0, 1)
    from_z(0, 2)
    along_z(1, 1)
    from_first(0, 0, True)
    from_first(0, 1, False)
    along_z(1, 0)
    from_second(0, 2)
    from_z(0, 3)
    from_first(0, 1, True)
    from_first(0, 2, False)
    from_second(0, 3)
    from_second(1, 0)
    from_z(1, 1)
    from_first(0, 2, True)
    from_first(0, 3, False)
    from_first(1, 0, False)
    from_second(1, 1)
    from_first(0, 3, True)
    from_z(1, 2)
    from_first(1, 0, True)
    for j in range(4):
        from_core(0, j)
    project(0, at.c)
    from_first(1, 1, False)
    from_second(1, 2)
    from_z(1, 3)
    from_first(1, 1, True)
    from_core(1, 0)
    project(0, 1 - at.c)
    project(1, at.c)
    from_first(1, 2, False)
    from_second(1, 3)
    from_core(1, 1)
    project(1, 1 - at.c)
    from_first(1, 2, True)
    project(2, at.c)
    from_first(1, 3, False)
    from_core(1, 2)
    project(2, 1 - at.c)
    from_first(1, 3, True)
    project(3, at.c)
    from_core(1, 3)
    project(3, 1 - at.c)

    slot_back[at.tok] = slot_out[at.tok]
    for n in range(4):
        span = slice(n * CAP, (n + 1) * CAP)
        asked = members[:, span, :].reshape(16 * CAP, tokens)
        total = product(asked, slot_out[:, span, :].reshape(16 * CAP, panel), 0, 0)
        total += product(asked, low[:, span, :].reshape(16 * CAP, panel), 0, 0)
        totals_ref[:, n * panel : (n + 1) * panel] = total[:REQUESTS]
    for distance in range(1, 16):
        source = (at.tok + distance) % 16
        slot_copy(source, source).wait_recv()
    for layer in (0, 1):
        table = slot_back[:, layer * 2 * CAP : (layer + 1) * 2 * CAP, :].reshape(32 * CAP, panel)
        for k in (0, 1):
            scores_ref[2 * layer + k] = product(sent[2 * layer + k], table, 0, 0).astype(scores_ref.dtype)

    for distance in range(1, 16):
        target = (at.tok + distance) % 16
        code_copy(target, target).wait_send()
        slot_copy(target, target).wait_send()
    for j in range(4):
        for n in range(4):
            core_copy(j, n).wait_send()
    for w in range(WAVES):
        sample = grads.at[0, wave(w)]

        def done(sem):
            remote(sample, sample, sem, block_recv.at[w, 0], at.to_core).wait_send()

        for j in range(4):
            first_copy(w, j, 0).wait_send()
            first_copy(w, j, 1).wait_send()
            second_copy(w, j).wait_send()
            if j > 0:
                done(z_send.at[w, j])
        for i in range(16):
            done(own_core.at[w, i])
        for i in range(8):
            done(own_first.at[w, i])
        for i in range(4):
            done(own_second.at[w, i])

        @pl.when(at.z > 0)
        def _():
            done(own_z.at[w, 0])

        @pl.when(at.z < 3)
        def _():
            done(own_z.at[w, 1])

        @pl.when(at.inner)
        def _():
            for i in range(2, 5):
                done(own_z.at[w, i])


def transcoder(codes, ids, requests, limits, weights, target):
    layers, tokens, panel = codes.shape
    depth, width = weights.shape
    half = target.shape[0] // 2
    step = half // WAVES
    dma, bf16 = pltpu.SemaphoreType.DMA, jnp.bfloat16
    vmem, anywhere = pl.BlockSpec(memory_space=pltpu.VMEM), pl.BlockSpec(memory_space=pl.ANY)
    slots = 4 * CAP

    def room(*shape, kind=bf16):
        return pltpu.VMEM(shape, kind)

    return pl.pallas_call(
        transcoder_kernel,
        out_shape=(
            jax.ShapeDtypeStruct((layers, tokens, panel), bf16),
            jax.ShapeDtypeStruct((REQUESTS, depth), jnp.float32),
        ),
        in_specs=[vmem] * 4 + [anywhere] * 2,
        out_specs=(vmem, vmem),
        scratch_shapes=[
            room(depth, width), room(half, width), room(16, slots + 16, panel), room(16, slots + 16, panel),
            room(4, 32 * CAP, tokens), room(16, 2 * slots, tokens), room(8, tokens, tokens), room(16, slots, tokens),
            room(4, 2, slots, width), room(4, 2, 2 * slots, width), room(4, 2, half, width, kind=jnp.float32),
            room(4, 2, half, width), room(4, 2, half, width), room(4, half, width), room(4, half, width),
            room(4, half, width), room(8, half, width), room(32, half, width), room(4, 2 * CAP, width),
            room(16, slots, panel), room(16, slots, panel), room(16, slots, panel),
            dma((2,)), dma((16,)), dma((16,)), dma((4, 4)), dma((4, 4)), dma((WAVES, 4, 2)), dma((WAVES, 4, 2)),
            dma((WAVES, 4)), dma((WAVES, 4)), dma((WAVES, 4)), dma((WAVES, 8)), dma((WAVES, 16)), dma((WAVES, 8)),
            dma((WAVES, 4)), dma((WAVES, 5)), dma((WAVES, 32)), dma((16,)), dma((16,)),
        ],
        compiler_params=pltpu.CompilerParams(
            collective_id=1, has_side_effects=True, vmem_limit_bytes=60 * 1024 * 1024
        ),
        name="transcoder",
    )(codes, ids, requests, limits, weights, target)


def per_device(feature_codes, block_ids, target_layer, request_ids, target_resid, decoder, grid=False):
    layers_here, count, kact, panel = feature_codes.shape
    width = target_resid.shape[1]
    features = decoder.shape[1]
    per_dev = features // panel
    tok, lyr = lax.axis_index("tok"), lax.axis_index("lyr")
    lyr_count = lax.axis_size("lyr")
    layer_ids = lyr * layers_here + jnp.arange(layers_here, dtype=jnp.int32)
    alive = layer_ids[:, None] <= target_layer[None, :]
    masked = jnp.where(alive[:, :, None, None], feature_codes, jnp.zeros_like(feature_codes))
    numbers = jnp.concatenate(
        [jnp.moveaxis(block_ids, 1, 2).reshape(layers_here * kact, count), request_ids[None, :]], axis=0
    )
    weights = decoder.reshape(layers_here * features, width)
    rows = count // lyr_count
    resid = lax.dynamic_slice_in_dim(target_resid, lyr * rows, rows, 0)
    if grid:
        by_k = jnp.moveaxis(feature_codes, 1, 2).reshape(layers_here * kact, count, panel)
        ids = jnp.moveaxis(block_ids, 1, 2).reshape(layers_here * kact, count)
        scores, totals = transcoder(by_k, ids, request_ids[None, :], target_layer[None, :], weights, target_resid)
        scores = jnp.moveaxis(scores.reshape(layers_here, kact, count, panel), 1, 2)
        return (scores, totals.reshape(REQUESTS, layers_here, features))
    all_codes = lax.all_gather(masked, "tok", axis=1, tiled=True)
    numbers = lax.all_gather(numbers, "tok", axis=1, tiled=True)
    all_ids = jnp.moveaxis(numbers[:-1].reshape(layers_here, kact, -1), 1, 2)
    all_requests = numbers[-1]
    mine = tok * per_dev + jnp.arange(per_dev, dtype=jnp.int32)
    named = (all_ids[..., None] == mine).astype(jnp.bfloat16)
    dense = jnp.sum(all_codes[:, :, :, None, :] * named[..., None], axis=2)
    tokens = dense.shape[1]
    dense = jnp.swapaxes(dense, 0, 1).reshape(tokens, layers_here * features)
    partial = jnp.dot(dense, weights, preferred_element_type=jnp.float32).astype(jnp.bfloat16)
    rebuilt = lax.psum_scatter(partial, ("tok", "lyr"), scatter_dimension=0, tiled=True)
    error = resid.astype(jnp.float32) - rebuilt.astype(jnp.float32)
    spread = jnp.mean(error * error, axis=-1, keepdims=True)
    gradient = (error * lax.rsqrt(spread + 1e-06)).astype(jnp.bfloat16)
    gradients = lax.all_gather(gradient, ("tok", "lyr"), axis=0, tiled=True)
    projected = lax.dot_general(
        gradients, weights, (((1,), (1,)), ((), ())), preferred_element_type=jnp.float32
    ).astype(jnp.bfloat16)
    attribution = dense.astype(jnp.float32) * projected.astype(jnp.float32)
    members = (all_requests[:, None] == jnp.arange(REQUESTS, dtype=jnp.int32)).astype(jnp.float32)
    totals = lax.dot_general(
        members, attribution, (((0,), (0,)), ((), ())), precision=lax.Precision.HIGHEST
    ).reshape(REQUESTS, layers_here, features)
    scored = attribution.astype(jnp.bfloat16).reshape(tokens, layers_here, 1, per_dev, panel)
    spread_out = jnp.sum(
        scored * jnp.swapaxes(named, 0, 1)[..., None], axis=3
    )
    scores = lax.psum_scatter(
        jnp.swapaxes(spread_out, 0, 1), "tok", scatter_dimension=1, tiled=True
    )
    return (scores, totals)


def solution(mesh):
    placed = (
        P("lyr", "tok", None, None),
        P("lyr", "tok", None),
        P("tok"),
        P("tok"),
        P("tok", None),
        P("lyr", "tok", None),
    )
    wide = len({getattr(d, "coords", (0,))[0] for d in mesh.devices.flat})
    grid = (mesh.shape["tok"], mesh.shape["lyr"]) == (16, 2) and wide == 2
    return jax.shard_map(
        functools.partial(per_device, grid=grid),
        mesh=mesh,
        in_specs=placed,
        out_specs=(P("lyr", "tok", None, None), P(None, "lyr", "tok")),
        check_vma=False,
    )
```

time: 164 us -> 129 us (0.79)
  Pallas kernels: 154 us -> 122 us
  other arithmetic: 3.54 us -> 0 us
    pallas_call x2 -> x1, Pallas kernels: 154 us -> 122 us  [transcoder(): pl.pallas_call(transcoder_kernel, out_shape=(jax.ShapeDtypeStruct((layers...]
where the time goes in v1:
time: 129 us; the launch traced here: 127 us
  Pallas kernels  122 us (95%)
  local copies, waits for them, and re-layouts  5.13 us (4%)
    pallas_call x1, Pallas kernels, transcoder(): pl.pallas_call(transcoder_kernel, out_shape=(jax.ShapeDtypeStruct((layers...  122 us

profile of v1, /device:TPU:0, one launch (start us, length us, event | category | flops | bytes accessed | tf_op | source)
XLA Modules:
  0.0 127.4 jit_solution(6230477352018573700)
XLA Ops:
  0.6 1.7 %copy.8 = bf16[2,2,128,256]{3,2,1,0:T(8,128)(2,1)} copy(bf16[2,2,128,256]{3,1,2,0:T(2,128)(2,1)} %bitcast.14) | data formatting | bytes 524288 | tf_op jit(solution)/shard_map/transpose | solution.py:579
  2.3 121.7 %transcoder.1 = (bf16[4,128,256]{2,1,0:T(8,128)(2,1)}, f32[16,1024]{1,0:T(8,128)}) custom-call(bf16[4,128,256]{2,1,0:T(8,128)(2,1)} %bitcast.13, s32[4,128]{1,0:T(4,128)} %bitcast.17, s32[1,128]{1,0:T(1,128)} %bitcast.18, s32[1,128]{1,0:T(1,128)} %bitcast.19, bf16[1024,2304]{1,0:T(8,128)(2,1)} %bitcast.12, bf16[128,2304]{1,0:T(8,128)(2,1)} %target_ref.1), custom_call_target="tpu_custom_call" | custom-call | tf_op jit(solution)/shard_map/transcoder/pallas_call | solution.py:536
  124.0 1.9 %copy.11 = bf16[2,2,128,256]{3,1,2,0:T(2,128)(2,1)} copy(bf16[2,2,128,256]{3,2,1,0:T(8,128)(2,1)} %bitcast.16) | data formatting | bytes 524288 | tf_op jit(solution)/shard_map/reshape | solution.py:582
  125.9 1.5 %reshape.23 = f32[16,2,512]{2,1,0:T(2,128)} reshape(f32[16,1024]{1,0:T(8,128)} %get-tuple-element.5) | data formatting | bytes 131072 | tf_op jit(solution)/shard_map/reshape | solution.py:583

commit v2 on v1

--- a/solution.py
+++ b/solution.py
@@ -9,21 +9,34 @@
 
 REQUESTS = 16
 CAP = 16
-WAVES = 2
 MESH = pl.DeviceIdType.MESH
+
+
+WAVES = ((0, 32, False), (32, 16, True), (48, 8, False))
+LAST = (56, 8)
+
+
+class Route:
+    def __init__(self, at, c):
+        x, y, self.c = at.x, at.y, c
+        self.first = (1 - c) * y + c * x
+        self.second = (1 - c) * x + c * y
+        across_x, across_y = (at.tok + 2 - 4 * x, y), (at.tok, 1 - y)
+        self.to_first = tuple((1 - c) * a + c * b for a, b in zip(across_y, across_x))
+        self.to_second = tuple((1 - c) * a + c * b for a, b in zip(across_x, across_y))
+
+    def spot(self, flip_first, flip_second):
+        f = 1 - self.first if flip_first else self.first
+        s = 1 - self.second if flip_second else self.second
+        return (1 - self.c) * s + self.c * f, (1 - self.c) * f + self.c * s
 
 
 class Place:
     def __init__(self):
         tok, y = lax.axis_index("tok"), lax.axis_index("lyr")
         z, x, c = tok // 4, (tok // 2) % 2, tok % 2
-        self.z, self.c = z, c
+        self.z, self.x, self.c = z, x, c
         self.inner = (z % 3) != 0
-        self.first = (1 - c) * y + c * x
-        self.second = (1 - c) * x + c * y
-        across_x, across_y = (tok + 2 - 4 * x, y), (tok, 1 - y)
-        self.to_first = tuple((1 - c) * a + c * b for a, b in zip(across_y, across_x))
-        self.to_second = tuple((1 - c) * a + c * b for a, b in zip(across_x, across_y))
         self.to_core = (tok + 1 - 2 * c, y)
         self.tok, self.y = tok, y
         half = z // 2
@@ -31,9 +44,6 @@
 
     def along(self, step):
         return (self.tok + 4 * step, self.y)
-
-    def quarter(self, first, second):
-        return (1 - self.c) * (second * 2 + first) + self.c * (first * 2 + second)
 
     def peer(self, distance):
         return ((self.tok + distance) % 16, self.y)
@@ -76,10 +86,11 @@
 
 def transcoder_kernel(
     codes_ref, ids_ref, request_ref, limit_ref, decoder_ref, target_ref, scores_ref, totals_ref,
-    weights, resid, packed, slot_in, sent, hot, turned, members, core_out, chip_in, held,
+    weights, resid, packed, slot_in, sent, hot, turned, members, core_out, chip_in, held, final,
     first_out, first_in, second_out, second_in, z_out, z_in, grads, picked, slot_out, slot_back, low,
+    last_total, last_first_out, last_first_in, last_second_out, last_second_in, last_out, last_in,
     load_sem, code_send, code_recv, core_send, core_recv, first_send, first_recv, second_send, second_recv,
-    z_send, z_recv, own_core, own_first, own_second, own_z, block_recv, slot_send, slot_recv,
+    z_send, z_recv, own_core, own_first, own_second, own_z, block_recv, slot_send, slot_recv, last_send, last_recv,
 ):
     at = Place()
     at.greet()
@@ -87,7 +98,7 @@
     tokens = limit_ref.shape[1]
     panel = codes_ref.shape[-1]
     slots = 4 * CAP
-    step = half // WAVES
+    routes = [Route(at, 0 if flipped else at.c) for _, _, flipped in WAVES]
     tile = width // 3 if width % 384 == 0 else width
     tiles = [slice(t, t + tile) for t in range(0, width, tile)]
     load = pltpu.make_async_copy(decoder_ref, weights, load_sem.at[0])
@@ -98,7 +109,7 @@
     load_target.start()
 
     def wave(w):
-        return pl.ds(w * step, step)
+        return pl.ds(WAVES[w][0], WAVES[w][1])
 
     info = []
     ids = ids_ref[...]
@@ -194,35 +205,27 @@
                     chip_in[j, x, span, cols] = value[(2 + x) * CAP : (3 + x) * CAP]
             core_copy(j, n).start()
 
-    def spot(k):
-        return 1 - at.second if k == 0 else at.second
-
     def combine(j):
         for n in range(4):
             core_copy(j, n).wait_recv()
-        for kept in (False, True):
-            for k in (0, 1):
-                first = at.first if kept else 1 - at.first
-                x = (1 - at.c) * spot(k) + at.c * first
-                h = (1 - at.c) * first + at.c * spot(k)
-                left = turned[2 * j + x, pl.ds(pl.multiple_of(h * half, half), half), :]
-                for cols in tiles:
-                    value = product(left, chip_in[j, x, :, cols])
-                    if kept:
-                        held[j, k, :, cols] = value
-                    else:
-                        first_out[j, k, :, cols] = value.astype(first_out.dtype)
+        for x in (0, 1):
+            for cols in tiles:
+                held[j, x, :, cols] = product(turned[2 * j + x], chip_in[j, x, :, cols])
+
+    def kept(w, j, flip_first, flip_second):
+        x, h = routes[w].spot(flip_first, flip_second)
+        return held[j, x, pl.ds(pl.multiple_of(h * half + WAVES[w][0], 8), WAVES[w][1])]
 
     def first_copy(w, j, k):
         return remote(
             first_out.at[j, k, wave(w)], first_in.at[j, k, wave(w)], first_send.at[w, j, k], first_recv.at[w, j, k],
-            at.to_first,
+            routes[w].to_first,
         )
 
     def second_copy(w, j):
         return remote(
             second_out.at[j, wave(w)], second_in.at[j, wave(w)], second_send.at[w, j], second_recv.at[w, j],
-            at.to_second,
+            routes[w].to_second,
         )
 
     def z_arrived(w, slot):
@@ -232,18 +235,19 @@
 
     def over_first(w, j):
         for k in (0, 1):
+            first_out[j, k, wave(w)] = kept(w, j, True, k == 0).astype(first_out.dtype)
             first_copy(w, j, k).start()
 
     def over_second(w, j):
         first_copy(w, j, 0).wait_recv()
-        second_out[j, wave(w)] = (held[j, 0, wave(w)] + f32(first_in[j, 0, wave(w)])).astype(second_out.dtype)
+        second_out[j, wave(w)] = (kept(w, j, False, True) + f32(first_in[j, 0, wave(w)])).astype(second_out.dtype)
         second_copy(w, j).start()
 
     def along_z(w, j):
         rows = wave(w)
         first_copy(w, j, 1).wait_recv()
         second_copy(w, j).wait_recv()
-        total = held[j, 1, rows] + f32(first_in[j, 1, rows]) + f32(second_in[j, rows])
+        total = kept(w, j, False, False) + f32(first_in[j, 1, rows]) + f32(second_in[j, rows])
         if j > 0:
             way = (at.z // 2) if j > 1 else (at.z % 2)
             slot = way * 4 + at.near[j]
@@ -261,30 +265,29 @@
                 z_out.at[j, rows], z_in.at[slot, rows], z_send.at[w, j], z_recv.at[w, slot], at.along(1 - 2 * way)
             ).start()
         else:
-            held[j, 1, rows] = total
+            final[rows] = total
 
             @pl.when(at.z > 0)
             def _():
                 z_arrived(w, at.z)
-                held[j, 1, rows] += f32(z_in[at.z, rows])
+                final[rows] += f32(z_in[at.z, rows])
 
             @pl.when(at.z < 3)
             def _():
                 z_arrived(w, 4 + at.z)
-                held[j, 1, rows] += f32(z_in[4 + at.z, rows])
-
-            error = f32(resid[rows]) - held[j, 1, rows]
-            spread = jnp.mean(error * error, axis=-1, keepdims=True)
-            grads[mine(0, False, False), rows] = (error * lax.rsqrt(spread + 1e-06)).astype(grads.dtype)
+                final[rows] += f32(z_in[4 + at.z, rows])
+
+            grads[mine(w, 0, False, False), rows] = gradient(rows, final[rows])
             spread_out(w)
 
-    def block(z, first, second, core):
-        return (z * 2 + core) * 4 + at.quarter(first, second)
-
-    def mine(j, flip_first, flip_second):
-        f = 1 - at.first if flip_first else at.first
-        s = 1 - at.second if flip_second else at.second
-        return block(at.near[j], f, s, at.c)
+    def gradient(rows, rebuilt):
+        error = f32(resid[rows]) - rebuilt
+        spread = jnp.mean(error * error, axis=-1, keepdims=True)
+        return (error * lax.rsqrt(spread + 1e-06)).astype(grads.dtype)
+
+    def mine(w, j, flip_first, flip_second):
+        x, h = routes[w].spot(flip_first, flip_second)
+        return (at.near[j] * 2 + at.c) * 4 + x * 2 + h
 
     def send(w, b, sem, target):
         remote(grads.at[b, wave(w)], grads.at[b, wave(w)], sem, block_recv.at[w, b], target).start()
@@ -294,20 +297,20 @@
             grads.at[b, wave(w)], grads.at[b, wave(w)], own_core.at[w, 0], block_recv.at[w, b], at.to_core
         ).wait_recv()
 
-    used = [[0, 0, 0] for _ in range(WAVES)]
+    used = [[0, 0, 0] for _ in WAVES]
 
     def fan(w, b, second, first):
         if second:
-            send(w, b, own_second.at[w, used[w][1]], at.to_second)
+            send(w, b, own_second.at[w, used[w][1]], routes[w].to_second)
             used[w][1] += 1
         if first:
-            send(w, b, own_first.at[w, used[w][0]], at.to_first)
+            send(w, b, own_first.at[w, used[w][0]], routes[w].to_first)
             used[w][0] += 1
         send(w, b, own_core.at[w, used[w][2]], at.to_core)
         used[w][2] += 1
 
     def spread_out(w):
-        b = mine(0, False, False)
+        b = mine(w, 0, False, False)
 
         @pl.when(at.z > 0)
         def _():
@@ -320,7 +323,7 @@
         fan(w, b, True, True)
 
     def from_z(w, j):
-        b = mine(j, False, False)
+        b = mine(w, j, False, False)
         arrived(w, b)
         onward = (3 - 2 * at.z) if j == 1 else (2 * at.z - 3)
 
@@ -331,36 +334,154 @@
         fan(w, b, True, True)
 
     def from_second(w, j):
-        b = mine(j, False, True)
+        b = mine(w, j, False, True)
         arrived(w, b)
         fan(w, b, False, True)
 
     def from_first(w, j, flip):
-        b = mine(j, True, flip)
+        b = mine(w, j, True, flip)
         arrived(w, b)
         fan(w, b, False, False)
 
     def from_core(w, j):
         for q in range(4):
             arrived(w, (at.near[j] * 2 + 1 - at.c) * 4 + q)
+
+    last = pl.ds(LAST[0], LAST[1])
+    route = Route(at, at.c)
+
+    def last_held(j, x, h):
+        return held[j, x, pl.ds(pl.multiple_of(h * half + LAST[0], 8), LAST[1])]
+
+    def last_along(way, slot, j, step):
+        return remote(last_out.at[j], last_in.at[slot], last_send.at[j], last_recv.at[slot], at.along(step))
+
+    def last_quarter(flip_first, flip_second):
+        x, h = route.spot(flip_first, flip_second)
+        return x * 2 + h
+
+    def last_over_first():
+        return remote(last_first_out, last_first_in, last_send.at[4], last_recv.at[8], route.to_first)
+
+    def last_over_second():
+        return remote(last_second_out, last_second_in, last_send.at[5], last_recv.at[9], route.to_second)
+
+    def last_z(j):
+        def come(slot):
+            remote(last_in.at[slot], last_in.at[slot], last_send.at[0], last_recv.at[slot], at.to_core).wait_recv()
+
+        if j > 0:
+            way = (at.z // 2) if j > 1 else (at.z % 2)
+            slot = way * 4 + at.near[j]
+
+            @pl.when(at.inner)
+            def _():
+                come(slot)
+                for q in range(4):
+                    last_out[j, q] = (last_held(j, q // 2, q % 2) + f32(last_in[slot, q])).astype(last_out.dtype)
+
+            @pl.when(jnp.logical_not(at.inner))
+            def _():
+                for q in range(4):
+                    last_out[j, q] = last_held(j, q // 2, q % 2).astype(last_out.dtype)
+
+            last_along(way, slot, j, 1 - 2 * way).start()
+        else:
+            for q in range(4):
+                last_total[q] = last_held(0, q // 2, q % 2)
+
+            @pl.when(at.z > 0)
+            def _():
+                come(at.z)
+                for q in range(4):
+                    last_total[q] += f32(last_in[at.z, q])
+
+            @pl.when(at.z < 3)
+            def _():
+                come(4 + at.z)
+                for q in range(4):
+                    last_total[q] += f32(last_in[4 + at.z, q])
+
+            for k in (0, 1):
+                last_first_out[k] = last_total[last_quarter(True, k == 0)].astype(last_out.dtype)
+            last_over_first().start()
+
+    def last_second():
+        last_over_first().wait_recv()
+        last_second_out[...] = (last_total[last_quarter(False, True)] + f32(last_first_in[0])).astype(last_out.dtype)
+        last_over_second().start()
+
+    def last_group(plane, core):
+        return grads.at[pl.ds((plane * 2 + core) * 4, 4), last]
+
+    def last_block(flip_first, flip_second):
+        return grads.at[(at.z * 2 + at.c) * 4 + last_quarter(flip_first, flip_second), last]
+
+    def last_pass(ref, sem, arrival, target):
+        return remote(ref, ref, last_send.at[sem], last_recv.at[arrival], target)
+
+    def last_final():
+        last_over_second().wait_recv()
+        total = last_total[last_quarter(False, False)] + f32(last_first_in[1]) + f32(last_second_in[...])
+        grads[(at.z * 2 + at.c) * 4 + last_quarter(False, False), last] = gradient(last, total)
+        own = last_block(False, False)
+        last_pass(own, 6, 10, route.to_second).start()
+        last_pass(own, 7, 11, route.to_first).start()
+
+    def last_from_second():
+        ref = last_block(False, True)
+        last_pass(ref, 6, 10, at.to_core).wait_recv()
+        last_pass(ref, 8, 12, route.to_first).start()
+
+    def last_from_first():
+        last_pass(last_block(True, False), 6, 11, at.to_core).wait_recv()
+        last_pass(last_block(True, True), 6, 12, at.to_core).wait_recv()
+        ref = last_group(at.z, at.c)
+
+        @pl.when(at.z > 0)
+        def _():
+            last_pass(ref, 9, 13 + at.z, at.along(-1)).start()
+
+        @pl.when(at.z < 3)
+        def _():
+            last_pass(ref, 10, 13 + at.z, at.along(1)).start()
+
+        last_pass(ref, 14, 17 + at.z, at.to_core).start()
+
+    def last_from_z(j):
+        ref = last_group(at.near[j], at.c)
+        last_pass(ref, 6, 13 + at.near[j], at.to_core).wait_recv()
+        onward = (3 - 2 * at.z) if j == 1 else (2 * at.z - 3)
+
+        @pl.when(at.inner)
+        def _():
+            last_pass(ref, 10 + j, 13 + at.near[j], at.along(onward)).start()
+
+        last_pass(ref, 14 + j, 17 + at.near[j], at.to_core).start()
+
+    def last_from_core(j):
+        last_pass(last_group(at.near[j], 1 - at.c), 6, 17 + at.near[j], at.to_core).wait_recv()
 
     def slot_copy(target, source):
         return remote(
             slot_out.at[target], slot_back.at[source], slot_send.at[target], slot_recv.at[source], (target, at.y)
         )
 
-    def pick(j, core):
-        for x in (0, 1):
-            source = at.near[j] * 4 + x * 2 + core
+    def place_of(j, core):
+        return [at.near[j] * 4 + x * 2 + core for x in (0, 1)]
+
+    def pick(j, away):
+        core = 1 - at.c if away else at.c
+        for x, source in enumerate(place_of(j, core)):
             rows = grads[pl.ds((at.near[j] * 2 + core) * 4 + 2 * x, 2)].reshape(tokens, width)
+            start = (2 * away + x) * CAP
             for cols in tiles:
                 value = product(hot[source, :slots, :], rows[:, cols]).astype(picked.dtype)
                 for n in range(4):
-                    picked[n, x * CAP : (x + 1) * CAP, cols] = value[n * CAP : (n + 1) * CAP]
-
-    def project(j, core):
-        pick(j, core)
-        sources = [at.near[j] * 4 + x * 2 + core for x in (0, 1)]
+                    picked[n, start : start + CAP, cols] = value[n * CAP : (n + 1) * CAP]
+
+    def project(j):
+        sources = place_of(j, at.c) + place_of(j, 1 - at.c)
 
         @pl.loop(0, 4)
         def _(n):
@@ -369,12 +490,12 @@
             value = value * f32(jnp.concatenate([slot_in[s, span, :] for s in sources], axis=0))
             high = value.astype(jnp.bfloat16)
             rest = (value - f32(high)).astype(jnp.bfloat16)
-            for x in (0, 1):
-                slot_out[sources[x], span, :] = high[x * CAP : (x + 1) * CAP]
-                low[sources[x], span, :] = rest[x * CAP : (x + 1) * CAP]
-
-        for source in sources:
-            if j == 0:
+            for i, source in enumerate(sources):
+                slot_out[source, span, :] = high[i * CAP : (i + 1) * CAP]
+                low[source, span, :] = rest[i * CAP : (i + 1) * CAP]
+
+        for i, source in enumerate(sources):
+            if j == 0 and i < 2:
 
                 @pl.when(source != at.tok)
                 def _():
@@ -387,84 +508,136 @@
     load.wait()
     contribute(0)
     combine(0)
-    for w in range(WAVES):
-        over_first(w, 0)
+    over_first(0, 0)
+    over_first(1, 0)
     unpack(3)
     contribute(3)
     combine(3)
     over_first(0, 3)
+    last_z(3)
     over_second(0, 0)
     unpack(2)
     contribute(2)
     combine(2)
     over_first(0, 2)
+    last_z(2)
     over_second(0, 3)
     unpack(1)
     contribute(1)
     combine(1)
     over_first(0, 1)
-    load_target.wait()
-    over_first(1, 3)
+    last_z(1)
+    over_second(1, 0)
     over_second(0, 2)
     along_z(0, 3)
-    over_second(1, 0)
-    over_first(1, 2)
+    over_first(1, 3)
     over_second(0, 1)
     along_z(0, 2)
-    over_first(1, 1)
+    over_first(1, 2)
+    last_z(0)
     along_z(0, 1)
     over_second(1, 3)
+    over_first(1, 1)
+    last_second()
+    over_first(2, 0)
+    over_first(2, 3)
+    load_target.wait()
     along_z(0, 0)
     over_second(1, 2)
+    last_final()
     along_z(1, 3)
+    over_first(2, 2)
+    over_first(2, 1)
+    over_second(1, 1)
+    along_z(1, 2)
+    over_second(2, 0)
+    over_second(2, 3)
     from_second(0, 0)
     from_z(0, 1)
-    over_second(1, 1)
-    along_z(1, 2)
+    last_from_second()
+    along_z(1, 1)
+    over_second(2, 2)
+    along_z(2, 3)
     from_first(0, 0, False)
     from_second(0, 1)
     from_z(0, 2)
-    along_z(1, 1)
+    along_z(1, 0)
+    over_second(2, 1)
+    along_z(2, 2)
+    last_from_first()
     from_first(0, 0, True)
     from_first(0, 1, False)
-    along_z(1, 0)
     from_second(0, 2)
     from_z(0, 3)
+    along_z(2, 1)
+    along_z(2, 0)
+    from_second(1, 0)
+    from_z(1, 1)
     from_first(0, 1, True)
     from_first(0, 2, False)
     from_second(0, 3)
-    from_second(1, 0)
-    from_z(1, 1)
+    last_from_z(1)
+    from_z(1, 2)
+    from_second(1, 1)
     from_first(0, 2, True)
     from_first(0, 3, False)
+    from_second(2, 0)
+    from_z(2, 1)
     from_first(1, 0, False)
-    from_second(1, 1)
+    last_from_z(2)
+    from_z(1, 3)
+    from_second(1, 2)
     from_first(0, 3, True)
-    from_z(1, 2)
     from_first(1, 0, True)
-    for j in range(4):
-        from_core(0, j)
-    project(0, at.c)
+    from_second(2, 1)
+    from_z(2, 2)
+    last_from_z(3)
     from_first(1, 1, False)
-    from_second(1, 2)
-    from_z(1, 3)
+    from_second(1, 3)
     from_first(1, 1, True)
+    from_z(2, 3)
+    from_second(2, 2)
+    from_first(1, 2, False)
+    from_first(2, 0, False)
+    from_first(2, 0, True)
+    from_first(1, 2, True)
+    from_second(2, 3)
+    from_core(0, 0)
     from_core(1, 0)
-    project(0, 1 - at.c)
-    project(1, at.c)
-    from_first(1, 2, False)
-    from_second(1, 3)
+    from_core(2, 0)
+    last_from_core(0)
+    pick(0, False)
+    pick(0, True)
+    from_first(1, 3, False)
+    from_first(1, 3, True)
+    from_first(2, 1, False)
+    project(0)
+    from_first(2, 1, True)
+    from_first(2, 2, False)
+    from_first(2, 2, True)
+    from_core(0, 1)
     from_core(1, 1)
-    project(1, 1 - at.c)
-    from_first(1, 2, True)
-    project(2, at.c)
-    from_first(1, 3, False)
+    from_core(2, 1)
+    last_from_core(1)
+    pick(1, False)
+    pick(1, True)
+    from_first(2, 3, False)
+    from_first(2, 3, True)
+    project(1)
+    from_core(0, 2)
     from_core(1, 2)
-    project(2, 1 - at.c)
-    from_first(1, 3, True)
-    project(3, at.c)
+    from_core(2, 2)
+    last_from_core(2)
+    pick(2, False)
+    pick(2, True)
+    project(2)
+    pick(3, False)
+    from_core(0, 3)
     from_core(1, 3)
-    project(3, 1 - at.c)
+    from_core(2, 3)
+    last_from_core(3)
+    pick(3, True)
+    project(3)
 
     slot_back[at.tok] = slot_out[at.tok]
     for n in range(4):
@@ -488,7 +661,7 @@
     for j in range(4):
         for n in range(4):
             core_copy(j, n).wait_send()
-    for w in range(WAVES):
+    for w in range(len(WAVES)):
         sample = grads.at[0, wave(w)]
 
         def done(sem):
@@ -521,11 +694,35 @@
                 done(own_z.at[w, i])
 
 
+    last_over_first().wait_send()
+    last_over_second().wait_send()
+    for j in range(1, 4):
+        last_pass(last_out.at[j], j, 0, at.to_core).wait_send()
+    one, four = last_block(False, False), last_group(at.z, at.c)
+    for i in (6, 7, 8):
+        last_pass(one, i, 10, at.to_core).wait_send()
+    for i in range(14, 18):
+        last_pass(four, i, 10, at.to_core).wait_send()
+
+    @pl.when(at.z > 0)
+    def _():
+        last_pass(four, 9, 10, at.to_core).wait_send()
+
+    @pl.when(at.z < 3)
+    def _():
+        last_pass(four, 10, 10, at.to_core).wait_send()
+
+    @pl.when(at.inner)
+    def _():
+        for i in range(11, 14):
+            last_pass(four, i, 10, at.to_core).wait_send()
+
+
 def transcoder(codes, ids, requests, limits, weights, target):
     layers, tokens, panel = codes.shape
     depth, width = weights.shape
     half = target.shape[0] // 2
-    step = half // WAVES
+    waves, quick = len(WAVES), LAST[1]
     dma, bf16 = pltpu.SemaphoreType.DMA, jnp.bfloat16
     vmem, anywhere = pl.BlockSpec(memory_space=pltpu.VMEM), pl.BlockSpec(memory_space=pl.ANY)
     slots = 4 * CAP
@@ -544,13 +741,16 @@
         scratch_shapes=[
             room(depth, width), room(half, width), room(16, slots + 16, panel), room(16, slots + 16, panel),
             room(4, 32 * CAP, tokens), room(16, 2 * slots, tokens), room(8, tokens, tokens), room(16, slots, tokens),
-            room(4, 2, slots, width), room(4, 2, 2 * slots, width), room(4, 2, half, width, kind=jnp.float32),
-            room(4, 2, half, width), room(4, 2, half, width), room(4, half, width), room(4, half, width),
-            room(4, half, width), room(8, half, width), room(32, half, width), room(4, 2 * CAP, width),
+            room(4, 2, slots, width), room(4, 2, 2 * slots, width), room(4, 2, tokens, width, kind=jnp.float32),
+            room(half, width, kind=jnp.float32), room(4, 2, half, width), room(4, 2, half, width), room(4, half, width), room(4, half, width),
+            room(4, half, width), room(8, half, width), room(32, half, width), room(4, 4 * CAP, width),
             room(16, slots, panel), room(16, slots, panel), room(16, slots, panel),
-            dma((2,)), dma((16,)), dma((16,)), dma((4, 4)), dma((4, 4)), dma((WAVES, 4, 2)), dma((WAVES, 4, 2)),
-            dma((WAVES, 4)), dma((WAVES, 4)), dma((WAVES, 4)), dma((WAVES, 8)), dma((WAVES, 16)), dma((WAVES, 8)),
-            dma((WAVES, 4)), dma((WAVES, 5)), dma((WAVES, 32)), dma((16,)), dma((16,)),
+            room(4, quick, width, kind=jnp.float32), room(2, quick, width), room(2, quick, width), room(quick, width),
+            room(quick, width), room(4, 4, quick, width), room(8, 4, quick, width),
+            dma((2,)), dma((16,)), dma((16,)), dma((4, 4)), dma((4, 4)), dma((waves, 4, 2)), dma((waves, 4, 2)),
+            dma((waves, 4)), dma((waves, 4)), dma((waves, 4)), dma((waves, 8)), dma((waves, 16)), dma((waves, 8)),
+            dma((waves, 4)), dma((waves, 5)), dma((waves, 32)), dma((16,)), dma((16,)),
+            dma((18,)), dma((21,)),
         ],
         compiler_params=pltpu.CompilerParams(
             collective_id=1, has_side_effects=True, vmem_limit_bytes=60 * 1024 * 1024

time: 129 us -> 133 us (1.031); the launches traced: 127 us -> 133 us
  Pallas kernels: 122 us -> 127 us
    pallas_call x1, Pallas kernels: 122 us -> 127 us  [transcoder(): pl.pallas_call(transcoder_kernel, out_shape=(jax.ShapeDtypeStruct((layers...]
where the time goes in v2:
time: 133 us
  Pallas kernels  127 us (95%)
  local copies, waits for them, and re-layouts  5.13 us (4%)
    pallas_call x1, Pallas kernels, transcoder(): pl.pallas_call(transcoder_kernel, out_shape=(jax.ShapeDtypeStruct((layers...  127 us

profile of v2, /device:TPU:0, one launch (start us, length us, event | category | flops | bytes accessed | tf_op | source)
XLA Modules:
  0.0 133.1 jit_solution(10885298543617226411)
XLA Ops:
  0.6 1.7 %copy.8 = bf16[2,2,128,256]{3,2,1,0:T(8,128)(2,1)} copy(bf16[2,2,128,256]{3,1,2,0:T(2,128)(2,1)} %bitcast.14) | data formatting | bytes 524288 | tf_op jit(solution)/shard_map/transpose | solution.py:779
  2.3 127.4 %transcoder.1 = (bf16[4,128,256]{2,1,0:T(8,128)(2,1)}, f32[16,1024]{1,0:T(8,128)}) custom-call(bf16[4,128,256]{2,1,0:T(8,128)(2,1)} %bitcast.13, s32[4,128]{1,0:T(4,128)} %bitcast.17, s32[1,128]{1,0:T(1,128)} %bitcast.18, s32[1,128]{1,0:T(1,128)} %bitcast.19, bf16[1024,2304]{1,0:T(8,128)(2,1)} %bitcast.12, bf16[128,2304]{1,0:T(8,128)(2,1)} %target_ref.1), custom_call_target="tpu_custom_call" | custom-call | tf_op jit(solution)/shard_map/transcoder/pallas_call | solution.py:733
  129.7 1.9 %copy.11 = bf16[2,2,128,256]{3,1,2,0:T(2,128)(2,1)} copy(bf16[2,2,128,256]{3,2,1,0:T(8,128)(2,1)} %bitcast.16) | data formatting | bytes 524288 | tf_op jit(solution)/shard_map/reshape | solution.py:782
  131.6 1.5 %reshape.23 = f32[16,2,512]{2,1,0:T(2,128)} reshape(f32[16,1024]{1,0:T(8,128)} %get-tuple-element.5) | data formatting | bytes 131072 | tf_op jit(solution)/shard_map/reshape | solution.py:783
